TPU v7x, 32 devices: a whole 2x2x4 slice. The times are simulated.
32 devices in a mesh: ulysses: 4 (over z), blk: 2 (over y), tensor: 4 (over x, core).
Axes of the slice: x: 2, y: 2, z: 4, core: 2. Of those that a mesh axis runs over, the one named last changes fastest.
Arguments:
- tokens: bfloat16 [2048, 5120], P(('ulysses', 'blk'), 'tensor'), may hold values from -20 to 20
- w_qkv: bfloat16 [5120, 3, 4096], P(None, None, ('ulysses', 'tensor')), may hold values from -2 to 2
- qkv_scale: float32 [3, 32], P(None, ('ulysses', 'tensor')), may hold values from 0.6 to 9
- block_mask: int32 [32, 16, 16], P(('ulysses', 'tensor')), may hold values from 0 to 1, as said below
- w_out: bfloat16 [4, 1024, 5120], P(None, 'tensor'), may hold values from -0.125 to 0.125
Outputs:
- mixed: bfloat16 [2048, 5120], P(('ulysses', 'blk'), 'tensor')
Inputs may be any that keep to these rules, and one draw needn't show every extreme that they name: `block_mask`: 0 or 1; the share of ones differs from head to head.
All inputs are finite; a program needn't handle non-finite values.
Results may differ from a plain program's by a relative error of at most 0.015.
Values may be sent and summed in bfloat16 or wider, within the bound.
A program may use at most 128 MiB of HBM per device.

v0:
```python
import math
import jax
import jax.numpy as jnp
from jax import lax
from jax.sharding import PartitionSpec as P


def local(tokens, w_qkv, qkv_scale, block_mask, w_out):
    group_count = lax.axis_size("ulysses")
    tensor_count = lax.axis_size("tensor")
    cycle_count = lax.axis_size("blk")
    tok_rows, feat_cols = tokens.shape
    width_all, triple, head_cols = w_qkv.shape
    heads_here = qkv_scale.shape[1]
    head_dim = head_cols // heads_here
    blocks_all = block_mask.shape[1]
    group_rows = tok_rows * group_count
    block_rows = cycle_count * group_rows // blocks_all
    start_sum = jnp.zeros((group_count, tok_rows, triple, head_cols), jnp.float32)
    pieces = lax.all_gather(tokens[None], ("ulysses", "tensor"), axis=0, tiled=True)

    def one_shard(which, accum):
        group_id = which // tensor_count
        feature_id = which % tensor_count
        weights = lax.dynamic_slice_in_dim(w_qkv, feature_id * feat_cols, feat_cols, 0)
        token_part = lax.dynamic_index_in_dim(pieces, which, 0, keepdims=False)
        product = jnp.einsum("rd,dcn->rcn", token_part, weights, preferred_element_type=jnp.float32)
        current = lax.dynamic_index_in_dim(accum, group_id, 0, keepdims=False)
        return lax.dynamic_update_index_in_dim(accum, current + product, group_id, 0)

    projected = lax.fori_loop(0, pieces.shape[0], one_shard, start_sum)
    projected = (
        projected.reshape(group_rows, triple, heads_here, head_dim) * qkv_scale[None, :, :, None]
    )
    projected = projected.astype(jnp.bfloat16)
    queries = projected[:, 0]
    keys = projected[:, 1]
    values = projected[:, 2]
    cycle_index = lax.axis_index("blk")
    local_rows = jnp.arange(group_rows, dtype=jnp.int32)
    query_pos = (
        local_rows // tok_rows * cycle_count + cycle_index
    ) * tok_rows + local_rows % tok_rows
    query_block = query_pos // block_rows
    block_ids = jnp.arange(blocks_all, dtype=jnp.int32)
    query_onehot = (query_block[:, None] == block_ids[None, :]).astype(jnp.bfloat16)
    query_live = jnp.einsum(
        "qn,hnm->hqm",
        query_onehot,
        block_mask.astype(jnp.bfloat16),
        preferred_element_type=jnp.float32,
    ).astype(jnp.bfloat16)
    score_scale = 1.0 / math.sqrt(head_dim)
    start_state = (
        jnp.full((heads_here, group_rows), -1e30, jnp.float32),
        jnp.zeros((heads_here, group_rows), jnp.float32),
        jnp.zeros((heads_here, group_rows, head_dim), jnp.float32),
    )
    key_all = lax.all_gather(keys, "blk", axis=0, tiled=True)
    value_all = lax.all_gather(values, "blk", axis=0, tiled=True)

    def one_block(which, state):
        highest, denominator, numerator = state
        key_part = lax.dynamic_slice_in_dim(key_all, which * group_rows, group_rows, 0)
        value_part = lax.dynamic_slice_in_dim(value_all, which * group_rows, group_rows, 0)
        gathered_row = which * group_rows + local_rows
        owner_cycle = gathered_row // group_rows
        inner_row = gathered_row % group_rows
        key_pos = (
            inner_row // tok_rows * cycle_count + owner_cycle
        ) * tok_rows + inner_row % tok_rows
        key_block = key_pos // block_rows
        key_onehot = (key_block[:, None] == block_ids[None, :]).astype(jnp.bfloat16)
        allowed = (
            jnp.einsum("hqn,kn->hqk", query_live, key_onehot, preferred_element_type=jnp.float32)
            > 0.5
        )
        allowed = allowed | (query_block[:, None] == key_block[None, :])[None]
        scores = (
            jnp.einsum("qhd,khd->hqk", queries, key_part, preferred_element_type=jnp.float32)
            * score_scale
        )
        scores = jnp.where(allowed, scores, -jnp.inf)
        new_high = jnp.maximum(highest, jnp.max(scores, axis=-1))
        weights = jnp.exp(scores - new_high[..., None])
        factor = jnp.exp(highest - new_high)
        denominator = denominator * factor + jnp.sum(weights, axis=-1)
        numerator = numerator * factor[..., None] + jnp.einsum(
            "hqk,khd->hqd",
            weights.astype(jnp.bfloat16),
            value_part,
            preferred_element_type=jnp.float32,
        )
        return (new_high, denominator, numerator)

    highest, denominator, numerator = lax.fori_loop(
        0, key_all.shape[0] // group_rows, one_block, start_state
    )
    attended = (numerator / denominator[..., None]).astype(jnp.bfloat16)
    grouped = attended.reshape(heads_here, group_count, tok_rows, head_dim)
    arrived = lax.all_to_all(grouped, "ulysses", split_axis=1, concat_axis=0, tiled=True)
    out_rows = w_out.reshape(group_count * heads_here, head_dim, w_out.shape[2])
    partial_value = jnp.einsum(
        "grd,gdf->rf", arrived[:, 0], out_rows, preferred_element_type=jnp.float32
    )
    summed = lax.psum_scatter(
        partial_value.astype(jnp.bfloat16), "tensor", scatter_dimension=1, tiled=True
    )
    return summed


def solution(mesh):
    return jax.shard_map(
        local,
        mesh=mesh,
        in_specs=(
            P(("ulysses", "blk"), "tensor"),
            P(None, None, ("ulysses", "tensor")),
            P(None, ("ulysses", "tensor")),
            P(("ulysses", "tensor"), None, None),
            P(None, "tensor", None),
        ),
        out_specs=P(("ulysses", "blk"), "tensor"),
        check_vma=False,
    )
```

profile of v0, /device:TPU:0, one launch (start us, length us, event | category | flops | bytes accessed | tf_op | source)
XLA Modules:
  0.0 308.4 jit_solution(13720380740776168870)
XLA Ops:
  8.1 91.8 %all-gather.7.cloned.1.call-done = bf16[4096,1280]{1,0:T(8,128)(2,1)} async-done(((bf16[256,1280]{1,0:T(8,128)(2,1)}), bf16[4096,1280]{1,0:T(8,128)(2,1)}) %all-gather.7.cloned.1.call-update) | async-done | bytes 10485776 | tf_op jit(solution)/shard_map/all_gather | solution.py:20
  100.1 57.4 %while.36 = (s32[]{:T(128)}, f32[4,256,3,256]{3,1,0,2:T(8,128)S(1)}, bf16[16,256,1280]{2,1,0:T(8,128)(2,1)}, bf16[5120,3,256]{2,0,1:T(8,128)(2,1)}, s32[]{:T(128...) while((s32[]{:T(128)}, ...), condition=%wide.region_1.2_spmd, body=%wide.region_0.1_spmd.sunk | while | flops 503513120 | bytes 5768004 | solution.py:31
  108.3 2.6 fusion.106
  115.5 2.6 fusion.106
  119.1 2.6 fusion.106
  122.6 2.6 fusion.106
  126.2 2.6 fusion.106
  129.8 2.6 fusion.106
  133.4 2.6 fusion.106
  137.0 2.6 fusion.106
  144.2 2.6 fusion.106
  151.3 2.6 fusion.106
  157.6 3.0 reshape.217
  160.6 3.0 multiply_convert_fusion
  166.9 18.5 %all-gather.9.cloned.1.call-done = bf16[2048,1,2,128]{3,2,1,0:T(2,128)(2,1)} async-done(((bf16[1024,1,2,128]{3,2,1,0:T(2,128)(2,1)}), bf16[2048,1,2,128]{3,2,1,0:T(2,128)(2,1)}) %all-gather.9.cloned.1.call-update) | async-done | bytes 1048592 | tf_op jit(solution)/shard_map/all_gather | solution.py:59
  185.4 22.9 %all-gather.11.cloned.1.call-done = bf16[2048,1,2,128]{3,2,1,0:T(2,128)(2,1)} async-done(((bf16[1024,1,2,128]{3,2,1,0:T(2,128)(2,1)}), bf16[2048,1,2,128]{3,2,1,0:T(2,128)(2,1)}) %all-gather.11.cloned.1.call-update) | async-done | bytes 1048592 | tf_op jit(solution)/shard_map/all_gather | solution.py:60
  208.3 33.7 %while.37 = (s32[]{:T(128)}, f32[2,1024]{1,0:T(2,128)S(1)}, f32[2,1024]{1,0:T(2,128)S(1)}, f32[2,1024,128]{2,1,0:T(8,128)S(1)}, bf16[2,1024,16]{1,2,0:T(8,128)(2...) while((s32[]{:T(128)}, f32[2,1024]{1,0:T(2,128)S(1)}, ...), condition=%wide.region_5.6_spmd.clone, body=%wide.region_2.5_spmd.clone.sunk | while | flops 1161677824 | bytes 83579104 | solution.py:96
  212.2 4.8 %fusion.113 = (f32[2,1024]{1,0:T(2,128)S(1)}, f32[2,1024,1024]{1,2,0:T(8,128)}) fusion(bf16[1024,2,128]{2,0,1:T(8,128)(2,1)S(1)} %get-tuple-element.690, bf16[1024,2,128]{2,1,0:T(2,128)(2,1)S(1)} %get-tuple-element.614, pred[1024,1024]{0,1:T(8,128)(4,1)S(1)} %broadcast_compare_fusion.2, f32[1024,2,1024]{2,0,1:T(8,128)S(1)} %fusion.112), kind=kOutput, calls=%fused_computation.126.clone.1 | convolution fusion | flops 547354624 | bytes 18882560 | tf_op jit(solution)/shard_map/while/body/eval_jaxpr/qhd,khd->hqk/dot_general | solution.py:80
  217.0 4.7 %fusion.115 = f32[2,1024]{1,0:T(2,128)S(1)} fusion(f32[2,1024,1024]{1,2,0:T(8,128)} %get-tuple-element.618, f32[2,1024]{1,0:T(2,128)S(1)} %fusion.114), kind=kLoop, calls=%fused_computation.16.clone.1 | loop fusion | flops 4192256 | bytes 8404992 | tf_op jit(solution)/shard_map/while/body/eval_jaxpr/reduce_sum | solution.py:87
  229.0 4.8 %fusion.113 = (f32[2,1024]{1,0:T(2,128)S(1)}, f32[2,1024,1024]{1,2,0:T(8,128)}) fusion(bf16[1024,2,128]{2,0,1:T(8,128)(2,1)S(1)} %get-tuple-element.690, bf16[1024,2,128]{2,1,0:T(2,128)(2,1)S(1)} %get-tuple-element.614, pred[1024,1024]{0,1:T(8,128)(4,1)S(1)} %broadcast_compare_fusion.2, f32[1024,2,1024]{2,0,1:T(8,128)S(1)} %fusion.112), kind=kOutput, calls=%fused_computation.126.clone.1 | convolution fusion | flops 547354624 | bytes 18882560 | tf_op jit(solution)/shard_map/while/body/eval_jaxpr/qhd,khd->hqk/dot_general | solution.py:80
  233.8 4.7 %fusion.115 = f32[2,1024]{1,0:T(2,128)S(1)} fusion(f32[2,1024,1024]{1,2,0:T(8,128)} %get-tuple-element.618, f32[2,1024]{1,0:T(2,128)S(1)} %fusion.114), kind=kLoop, calls=%fused_computation.16.clone.1 | loop fusion | flops 4192256 | bytes 8404992 | tf_op jit(solution)/shard_map/while/body/eval_jaxpr/reduce_sum | solution.py:87
  242.3 18.7 %all_to_all.15 = bf16[2,4,256,128]{3,2,0,1:T(8,128)(2,1)S(1)} all-to-all(bf16[2,4,256,128]{3,2,0,1:T(8,128)(2,1)S(1)} %copy.27), channel_id=1, replica_groups=mesh['ulysses'=4,'blk'=2,'tensor'=4] {'ulysses'}, dimensions={1} | all-to-all | bytes 1048576 | tf_op jit(solution)/shard_map/all_to_all | solution.py:101
  261.1 8.1 %fusion.68 = bf16[256,5120]{1,0:T(8,128)(2,1)} fusion(bf16[8,256,128]{2,1,0:T(8,128)(2,1)S(1)} %bitcast.73, bf16[8,128,5120]{2,1,0:T(8,128)(2,1)} %bitcast.76), kind=kOutput, calls=%fused_computation.94 | convolution fusion | flops 2685665280 | bytes 13631488 | tf_op jit(solution)/shard_map/grd,gdf->rf/dot_general | solution.py:103
  269.2 32.7 %reduce-scatter.2.cloned.1.call-done = bf16[256,1280]{1,0:T(8,128)(2,1)} async-done(((bf16[256,5120]{1,0:T(8,128)(2,1)}), bf16[256,1280]{1,0:T(8,128)(2,1)}) %reduce-scatter.2.cloned.1.call-update) | async-done | bytes 655376 | tf_op jit(solution)/shard_map/reduce_scatter | solution.py:106
  (66 shorter events, 50.7 us)
Async XLA Ops:
  6.5 93.3 %all-gather.7.cloned.1.call-start = ((), (), s32[]{:S(2)}) async-start(), calls=%async_computation.3 | async-start | bytes 11141120 | tf_op jit(solution)/shard_map/all_gather | solution.py:20
  7.3 178.2 %all-gather.9.cloned.1.call-start = ((), (), s32[]{:S(2)}) async-start(), calls=%async_computation.4 | async-start | bytes 1572864 | tf_op jit(solution)/shard_map/all_gather | solution.py:59
  157.5 9.0 %copy-start.1 = (s32[2,16,16]{2,1,0:T(8,128)S(1)}, s32[2,16,16]{2,1,0:T(8,128)}, u32[]{:S(2)}) copy-start(s32[2,16,16]{2,1,0:T(8,128)} %param.12) | copy-start | bytes 6148
  165.7 42.6 %all-gather.11.cloned.1.call-start = ((), (), s32[]{:S(2)}) async-start(), calls=%async_computation.5 | async-start | bytes 1572864 | tf_op jit(solution)/shard_map/all_gather | solution.py:60
  166.5 135.4 %reduce-scatter.2.cloned.1.call-start = ((), (), s32[]{:S(2)}) async-start(), calls=%async_computation.2 | async-start | bytes 3276800 | tf_op jit(solution)/shard_map/reduce_scatter | solution.py:106
  217.0 5.8 %copy-start = (f32[2,1024,1024]{1,2,0:T(8,128)S(1)}, f32[2,1024,1024]{1,2,0:T(8,128)}, u32[]{:S(2)}) copy-start(f32[2,1024,1024]{1,2,0:T(8,128)} %get-tuple-element.618) | copy-start | bytes 25165828 | tf_op jit(solution)/shard_map/while
  233.8 5.8 %copy-start = (f32[2,1024,1024]{1,2,0:T(8,128)S(1)}, f32[2,1024,1024]{1,2,0:T(8,128)}, u32[]{:S(2)}) copy-start(f32[2,1024,1024]{1,2,0:T(8,128)} %get-tuple-element.618) | copy-start | bytes 25165828 | tf_op jit(solution)/shard_map/while
Sparse Core Ops, SparseCore 0:
  9.6 90.2 all-gather.6
  165.8 19.5 all-gather.8
  187.0 21.2 all-gather.10
  269.4 32.4 reduce-scatter.1
where the time goes:
time: 309 us; the launch traced here: 308 us
  waiting for transfers between devices  167 us (54%)
  matrix products  66.7 us (22%)
  local copies, waits for them, and re-layouts  27.4 us (9%)
  blocking collectives  18.7 us (6%)
  other arithmetic  14.2 us (5%)
  between operations  13.2 us (4%)
    all_gather x1, waiting for transfers between devices, local(): lax.all_gather(tokens[None], ('ulysses', 'tensor'), axis=0, tiled=True)  91.8 us
    dot_general x16, matrix products, one_shard(): jnp.einsum('rd,dcn->rcn', token_part, weights, preferred_element_type=jnp...  41.7 us
    reduce_scatter x1, waiting for transfers between devices, local(): lax.psum_scatter(partial_value.astype(jnp.bfloat16), 'tensor', scatter_di...  32.7 us
    all_gather x1, waiting for transfers between devices, local(): value_all = lax.all_gather(values, 'blk', axis=0, tiled=True)  22.9 us
    all_to_all x1, blocking collectives, local(): lax.all_to_all(grouped, 'ulysses', split_axis=1, concat_axis=0, tiled=True)  18.7 us
    all_gather x1, waiting for transfers between devices, local(): key_all = lax.all_gather(keys, 'blk', axis=0, tiled=True)  18.5 us
    dynamic_slice x16, local copies, waits for them, and re-layouts, one_shard(): current = lax.dynamic_index_in_dim(accum, group_id, 0, keepdims=False)  15.1 us
    dot_general x2, matrix products, one_block(): jnp.einsum('qhd,khd->hqk', queries, key_part, preferred_element_type=jnp....  9.53 us
  transfers between devices with their start and end apart: 4, of which 4 were waited for; matrix products, arithmetic and copies ran while one was open for 0% of the time, Pallas kernels for 0%

commit v1 on v0

--- a/solution.py
+++ b/solution.py
@@ -3,6 +3,23 @@
 import jax.numpy as jnp
 from jax import lax
 from jax.sharding import PartitionSpec as P
+
+
+def joined_along(blocks, dim):
+    blocks = jnp.moveaxis(blocks, 0, dim)
+    shape = blocks.shape
+    return blocks.reshape(*shape[:dim], shape[dim] * shape[dim + 1], *shape[dim + 2 :])
+
+
+def ring_gather(array, axis, dim):
+    peers = lax.axis_size(axis)
+    right = [(i, (i + 1) % peers) for i in range(peers)]
+    tiles = [array]
+    while len(tiles) < peers:
+        tiles.append(lax.ppermute(tiles[-1], axis, right))
+    index = lax.axis_index(axis)
+    tiles = jnp.stack(tiles)[(index - jnp.arange(peers)) % peers]
+    return joined_along(tiles, dim)
 
 
 def local(tokens, w_qkv, qkv_scale, block_mask, w_out):
@@ -17,7 +34,7 @@
     group_rows = tok_rows * group_count
     block_rows = cycle_count * group_rows // blocks_all
     start_sum = jnp.zeros((group_count, tok_rows, triple, head_cols), jnp.float32)
-    pieces = lax.all_gather(tokens[None], ("ulysses", "tensor"), axis=0, tiled=True)
+    pieces = ring_gather(tokens[None], ("ulysses", "tensor"), 0)
 
     def one_shard(which, accum):
         group_id = which // tensor_count

time: 309 us -> 418 us (1.35)
  waiting for transfers between devices: 167 us -> 247 us
  local copies, waits for them, and re-layouts: 27.4 us -> 55.9 us
    ppermute x0 -> x15, waiting for transfers between devices: none -> 173 us  [ring_gather(): tiles.append(lax.ppermute(tiles[-1], axis, right))]
    all_gather x1 -> x0, waiting for transfers between devices: 91.8 us -> none  [local(): lax.all_gather(tokens[None], ('ulysses', 'tensor'), axis=0, tiled=True)]
    unnamed x4 -> x21, local copies, waits for them, and re-layouts: 0.84 us -> 18.5 us
    gather x0 -> x1, local copies, waits for them, and re-layouts: none -> 9.75 us  [ring_gather(): tiles = jnp.stack(tiles)[(index - jnp.arange(peers)) % peers]]
  transfers between devices with their start and end apart: 4 -> 18, of which waited for: 4 -> 18; matrix products, arithmetic and copies ran while one was open for 0% -> 5% of each run, Pallas kernels for 0% -> 0%
where the time goes in v1:
time: 418 us
  waiting for transfers between devices  247 us (59%)
  matrix products  66.6 us (16%)
  local copies, waits for them, and re-layouts  55.9 us (13%)
  blocking collectives  18.7 us (4%)
  other arithmetic  14.2 us (3%)
  between operations  13.2 us (3%)
    ppermute x15, waiting for transfers between devices, ring_gather(): tiles.append(lax.ppermute(tiles[-1], axis, right))  173 us
    dot_general x16, matrix products, one_shard(): jnp.einsum('rd,dcn->rcn', token_part, weights, preferred_element_type=jnp...  41.7 us
    reduce_scatter x1, waiting for transfers between devices, local(): lax.psum_scatter(partial_value.astype(jnp.bfloat16), 'tensor', scatter_di...  32.7 us
    all_gather x1, waiting for transfers between devices, local(): value_all = lax.all_gather(values, 'blk', axis=0, tiled=True)  22.9 us
    all_to_all x1, blocking collectives, local(): lax.all_to_all(grouped, 'ulysses', split_axis=1, concat_axis=0, tiled=True)  18.7 us
    unnamed x21, local copies, waits for them, and re-layouts  18.5 us
    all_gather x1, waiting for transfers between devices, local(): key_all = lax.all_gather(keys, 'blk', axis=0, tiled=True)  17.8 us
    dynamic_slice x16, local copies, waits for them, and re-layouts, one_shard(): current = lax.dynamic_index_in_dim(accum, group_id, 0, keepdims=False)  15.3 us
  transfers between devices with their start and end apart: 18, of which 18 were waited for; matrix products, arithmetic and copies ran while one was open for 5% of the time, Pallas kernels for 0%

profile of v1, /device:TPU:0, one launch (start us, length us, event | category | flops | bytes accessed | tf_op | source)
XLA Modules:
  0.0 417.7 jit_solution(16990001223133629032)
XLA Ops:
  7.0 13.4 %collective-permute-done = bf16[1,256,1280]{2,1,0:T(8,128)(2,1)S(1)} collective-permute-done((bf16[1,256,1280]{2,1,0:T(8,128)(2,1)}, bf16[1,256,1280]{2,1,0:T(8,128)(2,1)S(1)}, u32[]{:S(2)}, u32[]{:S(2)}) %collective-permute-start) | collective-permute-done | bytes 655392 | tf_op jit(solution)/shard_map/ppermute | solution.py:19
  20.5 12.7 %collective-permute-done.1 = bf16[1,256,1280]{2,1,0:T(8,128)(2,1)S(1)} collective-permute-done((bf16[1,256,1280]{2,1,0:T(8,128)(2,1)S(1)}, bf16[1,256,1280]{2,1,0:T(8,128)(2,1)S(1)}, u32[]{:S(2)}, u32[]{:S(2)}) %collective-permute-start.1) | collective-permute-done | bytes 655392 | tf_op jit(solution)/shard_map/ppermute | solution.py:19
  33.2 12.7 %collective-permute-done.2 = bf16[1,256,1280]{2,1,0:T(8,128)(2,1)S(1)} collective-permute-done((bf16[1,256,1280]{2,1,0:T(8,128)(2,1)S(1)}, bf16[1,256,1280]{2,1,0:T(8,128)(2,1)S(1)}, u32[]{:S(2)}, u32[]{:S(2)}) %collective-permute-start.2) | collective-permute-done | bytes 655392 | tf_op jit(solution)/shard_map/ppermute | solution.py:19
  45.9 12.7 %collective-permute-done.3 = bf16[1,256,1280]{2,1,0:T(8,128)(2,1)S(1)} collective-permute-done((bf16[1,256,1280]{2,1,0:T(8,128)(2,1)S(1)}, bf16[1,256,1280]{2,1,0:T(8,128)(2,1)S(1)}, u32[]{:S(2)}, u32[]{:S(2)}) %collective-permute-start.3) | collective-permute-done | bytes 655392 | tf_op jit(solution)/shard_map/ppermute | solution.py:19
  58.6 12.7 %collective-permute-done.4 = bf16[1,256,1280]{2,1,0:T(8,128)(2,1)S(1)} collective-permute-done((bf16[1,256,1280]{2,1,0:T(8,128)(2,1)S(1)}, bf16[1,256,1280]{2,1,0:T(8,128)(2,1)S(1)}, u32[]{:S(2)}, u32[]{:S(2)}) %collective-permute-start.4) | collective-permute-done | bytes 655392 | tf_op jit(solution)/shard_map/ppermute | solution.py:19
  71.3 12.8 %collective-permute-done.5 = bf16[1,256,1280]{2,1,0:T(8,128)(2,1)} collective-permute-done((bf16[1,256,1280]{2,1,0:T(8,128)(2,1)S(1)}, bf16[1,256,1280]{2,1,0:T(8,128)(2,1)}, u32[]{:S(2)}, u32[]{:S(2)}) %collective-permute-start.5) | collective-permute-done | bytes 655392 | tf_op jit(solution)/shard_map/ppermute | solution.py:19
  84.1 12.9 %collective-permute-done.6 = bf16[1,256,1280]{2,1,0:T(8,128)(2,1)S(1)} collective-permute-done((bf16[1,256,1280]{2,1,0:T(8,128)(2,1)}, bf16[1,256,1280]{2,1,0:T(8,128)(2,1)S(1)}, u32[]{:S(2)}, u32[]{:S(2)}) %collective-permute-start.6) | collective-permute-done | bytes 655392 | tf_op jit(solution)/shard_map/ppermute | solution.py:19
  99.8 10.1 %collective-permute-done.7 = bf16[1,256,1280]{2,1,0:T(8,128)(2,1)} collective-permute-done((bf16[1,256,1280]{2,1,0:T(8,128)(2,1)S(1)}, bf16[1,256,1280]{2,1,0:T(8,128)(2,1)}, u32[]{:S(2)}, u32[]{:S(2)}) %collective-permute-start.7) | collective-permute-done | bytes 655392 | tf_op jit(solution)/shard_map/ppermute | solution.py:19
  111.6 11.2 %collective-permute-done.8 = bf16[1,256,1280]{2,1,0:T(8,128)(2,1)S(1)} collective-permute-done((bf16[1,256,1280]{2,1,0:T(8,128)(2,1)}, bf16[1,256,1280]{2,1,0:T(8,128)(2,1)S(1)}, u32[]{:S(2)}, u32[]{:S(2)}) %collective-permute-start.8) | collective-permute-done | bytes 655392 | tf_op jit(solution)/shard_map/ppermute | solution.py:19
  125.7 9.8 %collective-permute-done.9 = bf16[1,256,1280]{2,1,0:T(8,128)(2,1)S(1)} collective-permute-done((bf16[1,256,1280]{2,1,0:T(8,128)(2,1)S(1)}, bf16[1,256,1280]{2,1,0:T(8,128)(2,1)S(1)}, u32[]{:S(2)}, u32[]{:S(2)}) %collective-permute-start.9) | collective-permute-done | bytes 655392 | tf_op jit(solution)/shard_map/ppermute | solution.py:19
  138.3 9.9 %collective-permute-done.10 = bf16[1,256,1280]{2,1,0:T(8,128)(2,1)S(1)} collective-permute-done((bf16[1,256,1280]{2,1,0:T(8,128)(2,1)S(1)}, bf16[1,256,1280]{2,1,0:T(8,128)(2,1)S(1)}, u32[]{:S(2)}, u32[]{:S(2)}) %collective-permute-start.10) | collective-permute-done | bytes 655392 | tf_op jit(solution)/shard_map/ppermute | solution.py:19
  151.1 9.8 %collective-permute-done.11 = bf16[1,256,1280]{2,1,0:T(8,128)(2,1)S(1)} collective-permute-done((bf16[1,256,1280]{2,1,0:T(8,128)(2,1)S(1)}, bf16[1,256,1280]{2,1,0:T(8,128)(2,1)S(1)}, u32[]{:S(2)}, u32[]{:S(2)}) %collective-permute-start.11) | collective-permute-done | bytes 655392 | tf_op jit(solution)/shard_map/ppermute | solution.py:19
  162.7 10.9 %collective-permute-done.12 = bf16[1,256,1280]{2,1,0:T(8,128)(2,1)S(1)} collective-permute-done((bf16[1,256,1280]{2,1,0:T(8,128)(2,1)S(1)}, bf16[1,256,1280]{2,1,0:T(8,128)(2,1)S(1)}, u32[]{:S(2)}, u32[]{:S(2)}) %collective-permute-start.12) | collective-permute-done | bytes 655392 | tf_op jit(solution)/shard_map/ppermute | solution.py:19
  175.4 10.9 %collective-permute-done.13 = bf16[1,256,1280]{2,1,0:T(8,128)(2,1)S(1)} collective-permute-done((bf16[1,256,1280]{2,1,0:T(8,128)(2,1)S(1)}, bf16[1,256,1280]{2,1,0:T(8,128)(2,1)S(1)}, u32[]{:S(2)}, u32[]{:S(2)}) %collective-permute-start.13) | collective-permute-done | bytes 655392 | tf_op jit(solution)/shard_map/ppermute | solution.py:19
  188.1 10.9 %collective-permute-done.14 = bf16[1,256,1280]{2,1,0:T(8,128)(2,1)S(1)} collective-permute-done((bf16[1,256,1280]{2,1,0:T(8,128)(2,1)S(1)}, bf16[1,256,1280]{2,1,0:T(8,128)(2,1)S(1)}, u32[]{:S(2)}, u32[]{:S(2)}) %collective-permute-start.14) | collective-permute-done | bytes 655392 | tf_op jit(solution)/shard_map/ppermute | solution.py:19
  199.9 9.8 %gather_fusion = bf16[16,256,1280]{2,1,0:T(8,128)(2,1)} fusion(bf16[16,256,1280]{2,1,0:T(8,128)(2,1)} %bitcast.25, s32[1024]{0:T(1024)S(1)} %pad_clamp_fusion), kind=kCustom, calls=%fused_computation | custom fusion | bytes 20971584 | tf_op jit(solution)/shard_map/gather | solution.py:21
  209.9 57.5 %while.36 = (s32[]{:T(128)}, f32[4,256,3,256]{3,1,0,2:T(8,128)S(1)}, bf16[16,256,1280]{2,1,0:T(8,128)(2,1)}, bf16[5120,3,256]{2,0,1:T(8,128)(2,1)}, s32[]{:T(128...) while((s32[]{:T(128)}, ...), condition=%wide.region_1.2_spmd, body=%wide.region_0.1_spmd.sunk | while | flops 503513120 | bytes 5768004 | solution.py:48
  277.0 17.8 %all-gather.5.cloned.1.call-done = bf16[2048,1,2,128]{3,2,1,0:T(2,128)(2,1)} async-done(((bf16[1024,1,2,128]{3,2,1,0:T(2,128)(2,1)}), bf16[2048,1,2,128]{3,2,1,0:T(2,128)(2,1)}) %all-gather.5.cloned.1.call-update) | async-done | bytes 1048592 | tf_op jit(solution)/shard_map/all_gather | solution.py:76
  294.9 22.9 %all-gather.7.cloned.1.call-done = bf16[2048,1,2,128]{3,2,1,0:T(2,128)(2,1)} async-done(((bf16[1024,1,2,128]{3,2,1,0:T(2,128)(2,1)}), bf16[2048,1,2,128]{3,2,1,0:T(2,128)(2,1)}) %all-gather.7.cloned.1.call-update) | async-done | bytes 1048592 | tf_op jit(solution)/shard_map/all_gather | solution.py:77
  317.7 33.5 %while.37 = (s32[]{:T(128)}, f32[2,1024]{1,0:T(2,128)S(1)}, f32[2,1024]{1,0:T(2,128)S(1)}, f32[2,1024,128]{2,1,0:T(8,128)S(1)}, bf16[2,1024,16]{1,2,0:T(8,128)(2...) while((s32[]{:T(128)}, f32[2,1024]{1,0:T(2,128)S(1)}, ...), condition=%wide.region_5.6_spmd.clone, body=%wide.region_2.5_spmd.clone.sunk | while | flops 1161677824 | bytes 83579104 | solution.py:113
  321.6 4.8 %fusion.115 = (f32[2,1024]{1,0:T(2,128)S(1)}, f32[2,1024,1024]{1,2,0:T(8,128)}) fusion(bf16[1024,2,128]{2,0,1:T(8,128)(2,1)S(1)} %get-tuple-element.690, bf16[1024,2,128]{2,1,0:T(2,128)(2,1)S(1)} %get-tuple-element.614, pred[1024,1024]{0,1:T(8,128)(4,1)S(1)} %broadcast_compare_fusion.2, f32[1024,2,1024]{2,0,1:T(8,128)S(1)} %fusion.114), kind=kOutput, calls=%fused_computation.150.clone.1 | convolution fusion | flops 547354624 | bytes 18882560 | tf_op jit(solution)/shard_map/while/body/eval_jaxpr/qhd,khd->hqk/dot_general | solution.py:97
  351.6 18.7 %all_to_all.15 = bf16[2,4,256,128]{3,2,0,1:T(8,128)(2,1)S(1)} all-to-all(bf16[2,4,256,128]{3,2,0,1:T(8,128)(2,1)S(1)} %copy.27), channel_id=1, replica_groups=mesh['ulysses'=4,'blk'=2,'tensor'=4] {'ulysses'}, dimensions={1} | all-to-all | bytes 1048576 | tf_op jit(solution)/shard_map/all_to_all | solution.py:118
  370.4 8.1 %fusion.68 = bf16[256,5120]{1,0:T(8,128)(2,1)} fusion(bf16[8,256,128]{2,1,0:T(8,128)(2,1)S(1)} %bitcast.109, bf16[8,128,5120]{2,1,0:T(8,128)(2,1)} %bitcast.112), kind=kOutput, calls=%fused_computation.95 | convolution fusion | flops 2685665280 | bytes 13631488 | tf_op jit(solution)/shard_map/grd,gdf->rf/dot_general | solution.py:120
  378.5 32.7 %reduce-scatter.2.cloned.1.call-done = bf16[256,1280]{1,0:T(8,128)(2,1)} async-done(((bf16[256,5120]{1,0:T(8,128)(2,1)}), bf16[256,1280]{1,0:T(8,128)(2,1)}) %reduce-scatter.2.cloned.1.call-update) | async-done | bytes 655376 | tf_op jit(solution)/shard_map/reduce_scatter | solution.py:123
  (114 shorter events, 115.5 us)
Async XLA Ops:
  6.5 288.3 %all-gather.5.cloned.1.call-start = ((), (), s32[]{:S(2)}) async-start(), calls=%async_computation.3 | async-start | bytes 1572864 | tf_op jit(solution)/shard_map/all_gather | solution.py:76
  6.5 13.9 %collective-permute-start = (bf16[1,256,1280]{2,1,0:T(8,128)(2,1)}, bf16[1,256,1280]{2,1,0:T(8,128)(2,1)S(1)}, u32[]{:S(2)}, u32[]{:S(2)}) collective-permute-start(bf16[1,256,1280]{2,1,0:T(8,128)(2,1)} %bitcast.108), channel_id=1, source_target_pairs={{0,1},{1,2},{2,3},{3,8},{8,9},{9,10},{10,11},{11,16},{16,17},{17,1... | collective-permute-start | bytes 1966088 | tf_op jit(solution)/shard_map/ppermute | solution.py:19
  20.5 12.7 %collective-permute-start.1 = (bf16[1,256,1280]{2,1,0:T(8,128)(2,1)S(1)}, bf16[1,256,1280]{2,1,0:T(8,128)(2,1)S(1)}, u32[]{:S(2)}, u32[]{:S(2)}) collective-permute-start(bf16[1,256,1280]{2,1,0:T(8,128)(2,1)S(1)} %collective-permute-done), channel_id=1, source_target_pairs={{0,1},{1,2},{2,3},{3,8},{8,9},{9,10},{10,11},{11,16},{16,17},{17,1... | collective-permute-start | bytes 1966088 | tf_op jit(solution)/shard_map/ppermute | solution.py:19
  33.2 12.7 %collective-permute-start.2 = (bf16[1,256,1280]{2,1,0:T(8,128)(2,1)S(1)}, bf16[1,256,1280]{2,1,0:T(8,128)(2,1)S(1)}, u32[]{:S(2)}, u32[]{:S(2)}) collective-permute-start(bf16[1,256,1280]{2,1,0:T(8,128)(2,1)S(1)} %collective-permute-done.1), channel_id=1, source_target_pairs={{0,1},{1,2},{2,3},{3,8},{8,9},{9,10},{10,11},{11,16},{16,17},{17,1... | collective-permute-start | bytes 1966088 | tf_op jit(solution)/shard_map/ppermute | solution.py:19
  45.9 12.7 %collective-permute-start.3 = (bf16[1,256,1280]{2,1,0:T(8,128)(2,1)S(1)}, bf16[1,256,1280]{2,1,0:T(8,128)(2,1)S(1)}, u32[]{:S(2)}, u32[]{:S(2)}) collective-permute-start(bf16[1,256,1280]{2,1,0:T(8,128)(2,1)S(1)} %collective-permute-done.2), channel_id=1, source_target_pairs={{0,1},{1,2},{2,3},{3,8},{8,9},{9,10},{10,11},{11,16},{16,17},{17,1... | collective-permute-start | bytes 1966088 | tf_op jit(solution)/shard_map/ppermute | solution.py:19
  58.6 12.7 %copy-start.1 = (bf16[1,256,1280]{2,1,0:T(8,128)(2,1)}, bf16[1,256,1280]{2,1,0:T(8,128)(2,1)S(1)}, u32[]{:S(2)}) copy-start(bf16[1,256,1280]{2,1,0:T(8,128)(2,1)S(1)} %collective-permute-done.3) | copy-start | bytes 1966084
  58.6 12.7 %collective-permute-start.4 = (bf16[1,256,1280]{2,1,0:T(8,128)(2,1)S(1)}, bf16[1,256,1280]{2,1,0:T(8,128)(2,1)S(1)}, u32[]{:S(2)}, u32[]{:S(2)}) collective-permute-start(bf16[1,256,1280]{2,1,0:T(8,128)(2,1)S(1)} %collective-permute-done.3), channel_id=1, source_target_pairs={{0,1},{1,2},{2,3},{3,8},{8,9},{9,10},{10,11},{11,16},{16,17},{17,1... | collective-permute-start | bytes 1966088 | tf_op jit(solution)/shard_map/ppermute | solution.py:19
  71.3 12.8 %collective-permute-start.5 = (bf16[1,256,1280]{2,1,0:T(8,128)(2,1)S(1)}, bf16[1,256,1280]{2,1,0:T(8,128)(2,1)}, u32[]{:S(2)}, u32[]{:S(2)}) collective-permute-start(bf16[1,256,1280]{2,1,0:T(8,128)(2,1)S(1)} %collective-permute-done.4), channel_id=1, source_target_pairs={{0,1},{1,2},{2,3},{3,8},{8,9},{9,10},{10,11},{11,16},{16,17},{17,1... | collective-permute-start | bytes 1966088 | tf_op jit(solution)/shard_map/ppermute | solution.py:19
  84.1 12.9 %collective-permute-start.6 = (bf16[1,256,1280]{2,1,0:T(8,128)(2,1)}, bf16[1,256,1280]{2,1,0:T(8,128)(2,1)S(1)}, u32[]{:S(2)}, u32[]{:S(2)}) collective-permute-start(bf16[1,256,1280]{2,1,0:T(8,128)(2,1)} %collective-permute-done.5), channel_id=1, source_target_pairs={{0,1},{1,2},{2,3},{3,8},{8,9},{9,10},{10,11},{11,16},{16,17},{17,1... | collective-permute-start | bytes 1966088 | tf_op jit(solution)/shard_map/ppermute | solution.py:19
  97.0 12.8 %collective-permute-start.7 = (bf16[1,256,1280]{2,1,0:T(8,128)(2,1)S(1)}, bf16[1,256,1280]{2,1,0:T(8,128)(2,1)}, u32[]{:S(2)}, u32[]{:S(2)}) collective-permute-start(bf16[1,256,1280]{2,1,0:T(8,128)(2,1)S(1)} %collective-permute-done.6), channel_id=1, source_target_pairs={{0,1},{1,2},{2,3},{3,8},{8,9},{9,10},{10,11},{11,16},{16,17},{17,1... | collective-permute-start | bytes 1966088 | tf_op jit(solution)/shard_map/ppermute | solution.py:19
  109.8 12.9 %collective-permute-start.8 = (bf16[1,256,1280]{2,1,0:T(8,128)(2,1)}, bf16[1,256,1280]{2,1,0:T(8,128)(2,1)S(1)}, u32[]{:S(2)}, u32[]{:S(2)}) collective-permute-start(bf16[1,256,1280]{2,1,0:T(8,128)(2,1)} %collective-permute-done.7), channel_id=1, source_target_pairs={{0,1},{1,2},{2,3},{3,8},{8,9},{9,10},{10,11},{11,16},{16,17},{17,1... | collective-permute-start | bytes 1966088 | tf_op jit(solution)/shard_map/ppermute | solution.py:19
  122.8 12.7 %collective-permute-start.9 = (bf16[1,256,1280]{2,1,0:T(8,128)(2,1)S(1)}, bf16[1,256,1280]{2,1,0:T(8,128)(2,1)S(1)}, u32[]{:S(2)}, u32[]{:S(2)}) collective-permute-start(bf16[1,256,1280]{2,1,0:T(8,128)(2,1)S(1)} %collective-permute-done.8), channel_id=1, source_target_pairs={{0,1},{1,2},{2,3},{3,8},{8,9},{9,10},{10,11},{11,16},{16,17},{17,1... | collective-permute-start | bytes 1966088 | tf_op jit(solution)/shard_map/ppermute | solution.py:19
  135.5 12.7 %collective-permute-start.10 = (bf16[1,256,1280]{2,1,0:T(8,128)(2,1)S(1)}, bf16[1,256,1280]{2,1,0:T(8,128)(2,1)S(1)}, u32[]{:S(2)}, u32[]{:S(2)}) collective-permute-start(bf16[1,256,1280]{2,1,0:T(8,128)(2,1)S(1)} %collective-permute-done.9), channel_id=1, source_target_pairs={{0,1},{1,2},{2,3},{3,8},{8,9},{9,10},{10,11},{11,16},{16,17},{17,1... | collective-permute-start | bytes 1966088 | tf_op jit(solution)/shard_map/ppermute | solution.py:19
  148.2 12.7 %collective-permute-start.11 = (bf16[1,256,1280]{2,1,0:T(8,128)(2,1)S(1)}, bf16[1,256,1280]{2,1,0:T(8,128)(2,1)S(1)}, u32[]{:S(2)}, u32[]{:S(2)}) collective-permute-start(bf16[1,256,1280]{2,1,0:T(8,128)(2,1)S(1)} %collective-permute-done.10), channel_id=1, source_target_pairs={{0,1},{1,2},{2,3},{3,8},{8,9},{9,10},{10,11},{11,16},{16,17},{17,1... | collective-permute-start | bytes 1966088 | tf_op jit(solution)/shard_map/ppermute | solution.py:19
  160.9 12.7 %collective-permute-start.12 = (bf16[1,256,1280]{2,1,0:T(8,128)(2,1)S(1)}, bf16[1,256,1280]{2,1,0:T(8,128)(2,1)S(1)}, u32[]{:S(2)}, u32[]{:S(2)}) collective-permute-start(bf16[1,256,1280]{2,1,0:T(8,128)(2,1)S(1)} %collective-permute-done.11), channel_id=1, source_target_pairs={{0,1},{1,2},{2,3},{3,8},{8,9},{9,10},{10,11},{11,16},{16,17},{17,1... | collective-permute-start | bytes 1966088 | tf_op jit(solution)/shard_map/ppermute | solution.py:19
  173.6 12.7 %collective-permute-start.13 = (bf16[1,256,1280]{2,1,0:T(8,128)(2,1)S(1)}, bf16[1,256,1280]{2,1,0:T(8,128)(2,1)S(1)}, u32[]{:S(2)}, u32[]{:S(2)}) collective-permute-start(bf16[1,256,1280]{2,1,0:T(8,128)(2,1)S(1)} %collective-permute-done.12), channel_id=1, source_target_pairs={{0,1},{1,2},{2,3},{3,8},{8,9},{9,10},{10,11},{11,16},{16,17},{17,1... | collective-permute-start | bytes 1966088 | tf_op jit(solution)/shard_map/ppermute | solution.py:19
  186.3 12.7 %collective-permute-start.14 = (bf16[1,256,1280]{2,1,0:T(8,128)(2,1)S(1)}, bf16[1,256,1280]{2,1,0:T(8,128)(2,1)S(1)}, u32[]{:S(2)}, u32[]{:S(2)}) collective-permute-start(bf16[1,256,1280]{2,1,0:T(8,128)(2,1)S(1)} %collective-permute-done.13), channel_id=1, source_target_pairs={{0,1},{1,2},{2,3},{3,8},{8,9},{9,10},{10,11},{11,16},{16,17},{17,1... | collective-permute-start | bytes 1966088 | tf_op jit(solution)/shard_map/ppermute | solution.py:19
  267.4 9.2 %copy-start.2 = (s32[2,16,16]{2,1,0:T(8,128)S(1)}, s32[2,16,16]{2,1,0:T(8,128)}, u32[]{:S(2)}) copy-start(s32[2,16,16]{2,1,0:T(8,128)} %param.12) | copy-start | bytes 6148
  275.7 42.0 %all-gather.7.cloned.1.call-start = ((), (), s32[]{:S(2)}) async-start(), calls=%async_computation.4 | async-start | bytes 1572864 | tf_op jit(solution)/shard_map/all_gather | solution.py:77
  276.4 134.7 %reduce-scatter.2.cloned.1.call-start = ((), (), s32[]{:S(2)}) async-start(), calls=%async_computation.2 | async-start | bytes 3276800 | tf_op jit(solution)/shard_map/reduce_scatter | solution.py:123
  326.4 5.8 %copy-start = (f32[2,1024,1024]{1,2,0:T(8,128)S(1)}, f32[2,1024,1024]{1,2,0:T(8,128)}, u32[]{:S(2)}) copy-start(f32[2,1024,1024]{1,2,0:T(8,128)} %get-tuple-element.618) | copy-start | bytes 25165828 | tf_op jit(solution)/shard_map/while
  343.2 5.8 %copy-start = (f32[2,1024,1024]{1,2,0:T(8,128)S(1)}, f32[2,1024,1024]{1,2,0:T(8,128)}, u32[]{:S(2)}) copy-start(f32[2,1024,1024]{1,2,0:T(8,128)} %get-tuple-element.618) | copy-start | bytes 25165828 | tf_op jit(solution)/shard_map/while
Sparse Core Ops, SparseCore 0:
  275.8 19.0 all-gather.4
  296.4 21.2 all-gather.6
  378.6 32.4 reduce-scatter.1
